TPU v7x, 32 devices: a whole 2x2x4 slice. The times are simulated.
32 devices in a mesh: groups: 2 (over y), owner: 4 (over z), head: 2 (over x), rep: 2 (over core).
Axes of the slice: x: 2, y: 2, z: 4, core: 2. Of those that a mesh axis runs over, the one named last changes fastest.
Arguments:
- queries: bfloat16 [4096, 8, 512], P(('groups', 'owner', 'rep'), 'head'), parts along dimension 0, may hold values from -10 to 10
- cotangent: bfloat16 [4096, 8, 512], P(('groups', 'owner', 'rep'), 'head'), parts along dimension 0, may hold values from -6 to 6
- own_kv: bfloat16 [4096, 8, 256], P(('groups', 'owner', 'rep'), 'head'), parts along dimension 0, may hold values from -6 to 6
- tables: int32 [4096, 1], P(('groups', 'owner', 'rep')), parts along dimension 0, may hold values from 0 to 3; in each aligned block of 256 rows (0 to 255, 256 to 511, ...) at most 128 rows name the same one
- table_owner: int32 [8], P('groups'), parts along dimension 0, may hold values from 0 to 3, each once
- cache_keys: float32 [8, 8, 1024, 128], P(('groups', 'owner'), 'head', 'rep'), parts along dimension 0, may hold values from -10 to 10
- cache_values: float32 [8, 8, 1024, 128], P(('groups', 'owner'), 'head', 'rep'), parts along dimension 0, may hold values from -6 to 6
- first_moment: float32 [2, 8, 8, 1024, 128], P(None, ('groups', 'owner'), 'head', 'rep'), parts along dimension 1, may hold values from -0.75 to 0.75
- second_moment: float32 [2, 8, 8, 1024, 128], P(None, ('groups', 'owner'), 'head', 'rep'), parts along dimension 1, may hold values from 1e-06 to 0.1
Outputs:
- attended: bfloat16 [4096, 8, 512], P(('groups', 'owner', 'rep'), 'head'), parts along dimension 0
- new_keys: float32 [8, 8, 1024, 128], P(('groups', 'owner'), 'head', 'rep'), parts along dimension 0
- new_values: float32 [8, 8, 1024, 128], P(('groups', 'owner'), 'head', 'rep'), parts along dimension 0
- new_first: float32 [2, 8, 8, 1024, 128], P(None, ('groups', 'owner'), 'head', 'rep'), parts along dimension 1
- new_second: float32 [2, 8, 8, 1024, 128], P(None, ('groups', 'owner'), 'head', 'rep'), parts along dimension 1
There are 2 independent parts, one for each index of `groups`. A program takes and returns all parts, laid end to end along the dimension named above; each array names one. Nothing has to cross between parts.
Inputs may be any that keep to these rules, and one draw needn't show every extreme that they name: `tables`: in the rows of one reader device no table is named by more than 128 tokens, a bound that some block reaches. `table_owner`: each owner holds exactly one table.
All inputs are finite; a program needn't handle non-finite values.
Results may differ from a plain program's by a relative error of at most 0.0085.
Values may be sent and summed in bfloat16 or wider, within the bound.
A program may use at most 128 MiB of HBM per device.

v0:
```python
import jax
import jax.numpy as jnp
from jax import lax
from jax.sharding import PartitionSpec as P


def per_device(
    queries,
    cotangent,
    own_kv,
    tables,
    table_owner,
    cache_keys,
    cache_values,
    first_moment,
    second_moment,
):
    n_owner = lax.axis_size("owner")
    q_dev = queries.shape[0]
    heads = queries.shape[1]
    width = queries.shape[2]
    head_dim = own_kv.shape[2] // 2
    groups = width // head_dim
    cap = 2 * q_dev // n_owner
    scale = head_dim ** (-0.5)
    table_hit = tables == jnp.arange(table_owner.shape[0], dtype=jnp.int32)[None, :]
    dest = jnp.sum(jnp.where(table_hit, table_owner[None, :], 0), axis=1, dtype=jnp.int32)
    dest_hit = (dest[:, None] == jnp.arange(n_owner, dtype=jnp.int32)[None, :]).astype(jnp.int32)
    rank = jnp.sum(
        (jnp.cumsum(dest_hit, axis=0, dtype=jnp.int32) - dest_hit) * dest_hit,
        axis=1,
        dtype=jnp.int32,
    )
    place = dest * cap + rank

    def pack(x):
        return jnp.zeros((n_owner * cap,) + x.shape[1:], x.dtype).at[place].set(x)

    sent = (
        lax.all_to_all(pack(queries), "owner", split_axis=0, concat_axis=0, tiled=True),
        lax.all_to_all(pack(cotangent), "owner", split_axis=0, concat_axis=0, tiled=True),
        lax.all_to_all(pack(own_kv), "owner", split_axis=0, concat_axis=0, tiled=True),
    )
    key_half = cache_keys[0].astype(jnp.bfloat16)
    val_half = cache_values[0].astype(jnp.bfloat16)
    q_rows, c_rows, kv_rows = sent
    key_use, val_use = (
        lax.all_gather(key_half, "rep", axis=1, tiled=True),
        lax.all_gather(val_half, "rep", axis=1, tiled=True),
    )
    count = q_rows.shape[0]
    block = 512
    n_blocks = count // block
    q_four = q_rows.reshape(count, heads, groups, head_dim)
    c_four = c_rows.reshape(count, heads, groups, head_dim)
    kself = kv_rows[:, :, :head_dim]
    vself = kv_rows[:, :, head_dim:].astype(jnp.float32)
    q_blocks = q_four.reshape(n_blocks, block, heads, groups, head_dim)
    c_blocks = c_four.reshape(n_blocks, block, heads, groups, head_dim)

    def scores_of(q_block):
        return (
            jnp.einsum("nkgd,ksd->nkgs", q_block, key_use, preferred_element_type=jnp.float32)
            * scale
        )

    def stats(q_block):
        score = scores_of(q_block)
        local_top = jnp.max(score, axis=-1)
        return (local_top, jnp.sum(jnp.exp(score - local_top[..., None]), axis=-1))

    local_top, local_total = lax.map(stats, q_blocks)
    local_top = local_top.reshape(count, heads, groups)
    local_total = local_total.reshape(count, heads, groups)
    own = jnp.einsum("nkgd,nkd->nkg", q_four, kself, preferred_element_type=jnp.float32) * scale
    top = jnp.maximum(local_top, own)
    self_exp = jnp.exp(own - top)
    total = local_total * jnp.exp(local_top - top) + self_exp
    self_weight = (self_exp / total).astype(jnp.bfloat16).astype(jnp.float32)
    top_blocks = top.reshape(n_blocks, block, heads, groups)
    total_blocks = total.reshape(n_blocks, block, heads, groups)

    def weighted(args):
        q_block, top_block, total_block = args
        prob = jnp.exp(scores_of(q_block) - top_block[..., None]) / total_block[..., None]
        return jnp.einsum(
            "nkgs,ksd->nkgd", prob.astype(jnp.bfloat16), val_use, preferred_element_type=jnp.float32
        )

    out_part = lax.map(weighted, (q_blocks, top_blocks, total_blocks)).reshape(
        count, heads, groups, head_dim
    )
    out = out_part + self_weight[..., None] * vself[:, :, None, :]
    delta = jnp.sum(c_four.astype(jnp.float32) * out, axis=-1)
    delta_blocks = delta.reshape(n_blocks, block, heads, groups)

    def backward(carry, args):
        grad_keys, grad_values = carry
        q_block, c_block, top_block, total_block, delta_block = args
        prob = jnp.exp(scores_of(q_block) - top_block[..., None]) / total_block[..., None]
        weights = prob.astype(jnp.bfloat16)
        dprob = jnp.einsum("nkgd,ksd->nkgs", c_block, val_use, preferred_element_type=jnp.float32)
        dweights = (prob * (dprob - delta_block[..., None])).astype(jnp.bfloat16)
        grad_keys = grad_keys + jnp.einsum(
            "nkgs,nkgd->ksd", dweights, q_block, preferred_element_type=jnp.float32
        )
        grad_values = grad_values + jnp.einsum(
            "nkgs,nkgd->ksd", weights, c_block, preferred_element_type=jnp.float32
        )
        return ((grad_keys, grad_values), None)

    zeros_grad = jnp.zeros(key_use.shape, jnp.float32)
    (grad_keys, grad_values), unused = lax.scan(
        backward,
        (zeros_grad, zeros_grad),
        (q_blocks, c_blocks, top_blocks, total_blocks, delta_blocks),
    )
    grad_keys = grad_keys * scale
    answer_rows = out.astype(jnp.bfloat16).reshape(count, heads, width)
    grad_keys, grad_values = (
        lax.psum_scatter(grad_keys, "rep", scatter_dimension=1, tiled=True),
        lax.psum_scatter(grad_values, "rep", scatter_dimension=1, tiled=True),
    )
    returned = lax.all_to_all(answer_rows, "owner", split_axis=0, concat_axis=0, tiled=True)
    attended = returned[place]
    grad = jnp.stack([grad_keys, grad_values])[:, None]
    new_first = 0.9 * first_moment + 0.1 * grad
    new_second = 0.95 * second_moment + 0.05 * grad * grad
    params = jnp.stack([cache_keys, cache_values])
    updated = params - 0.02 * new_first / (jnp.sqrt(new_second) + 1e-08)
    return (attended, updated[0], updated[1], new_first, new_second)


def solution(mesh):
    in_specs = (
        P(("groups", "owner", "rep"), "head", None),
        P(("groups", "owner", "rep"), "head", None),
        P(("groups", "owner", "rep"), "head", None),
        P(("groups", "owner", "rep"), None),
        P("groups"),
        P(("groups", "owner"), "head", "rep", None),
        P(("groups", "owner"), "head", "rep", None),
        P(None, ("groups", "owner"), "head", "rep", None),
        P(None, ("groups", "owner"), "head", "rep", None),
    )
    out_specs = (
        P(("groups", "owner", "rep"), "head", None),
        P(("groups", "owner"), "head", "rep", None),
        P(("groups", "owner"), "head", "rep", None),
        P(None, ("groups", "owner"), "head", "rep", None),
        P(None, ("groups", "owner"), "head", "rep", None),
    )
    return jax.shard_map(
        per_device, mesh=mesh, in_specs=in_specs, out_specs=out_specs, check_vma=False
    )
```

profile of v0, /device:TPU:0, one launch (start us, length us, event | category | flops | bytes accessed | tf_op | source)
XLA Modules:
  0.0 318.7 jit_solution(9832093002231911585)
XLA Ops:
  9.6 1.2 broadcast_in_dim.36
  10.9 29.6 %scatter_fusion.1 = bf16[512,4,256]{2,1,0:T(4,128)(2,1)} fusion(bf16[512,4,256]{2,1,0:T(4,128)(2,1)} %broadcast_in_dim.36, s32[256]{0:T(256)S(1)} %bitcast.119, bf16[256,4,256]{2,1,0:T(4,128)(2,1)} %param.11), kind=kCustom, calls=%fused_computation.2 | custom fusion | bytes 1573888 | tf_op jit(solution)/shard_map/scatter | solution.py:37
  40.5 6.5 %all-to-all-start.1 = ((bf16[512,4,256]{2,1,0:T(4,128)(2,1)}), bf16[512,4,256]{2,1,0:T(4,128)(2,1)S(1)}, u32[]{:S(2)}, u32[]{:S(2)}) async-start(bf16[512,4,256]{2,1,0:T(4,128)(2,1)} %scatter_fusion.1), calls=%async_computation.1 | async-start | bytes 2097152 | tf_op jit(solution)/shard_map/all_to_all | solution.py:42
  47.0 1.9 broadcast.81.clone
  48.8 28.7 %scatter_fusion = bf16[512,4,512]{2,1,0:T(4,128)(2,1)} fusion(bf16[512,4,512]{2,1,0:T(4,128)(2,1)} %broadcast.81.clone, s32[256]{0:T(256)S(1)} %bitcast.120, bf16[256,4,512]{2,1,0:T(4,128)(2,1)S(1)} %copy-done.7), kind=kCustom, calls=%fused_computation.1 | custom fusion | bytes 3146752 | tf_op jit(solution)/shard_map/scatter | solution.py:37
  78.6 5.1 %all-to-all-start = ((bf16[512,4,512]{2,1,0:T(4,128)(2,1)}), bf16[512,4,512]{2,1,0:T(4,128)(2,1)S(1)}, u32[]{:S(2)}, u32[]{:S(2)}) async-start(bf16[512,4,512]{2,1,0:T(4,128)(2,1)} %scatter_fusion), calls=%async_computation | async-start | bytes 4194304 | tf_op jit(solution)/shard_map/all_to_all | solution.py:40
  84.6 2.2 copy.51
  86.9 1.9 broadcast.81.clone.1
  88.7 31.3 %scatter_fusion.2 = bf16[512,4,512]{2,1,0:T(4,128)(2,1)} fusion(bf16[512,4,512]{2,1,0:T(4,128)(2,1)} %broadcast.81.clone.1, s32[256]{0:T(256)S(1)} %bitcast.121, bf16[256,4,512]{2,1,0:T(4,128)(2,1)} %param.10), kind=kCustom, calls=%fused_computation.3 | custom fusion | bytes 3146752 | tf_op jit(solution)/shard_map/scatter | solution.py:37
  120.1 1.4 fusion.35
  121.5 1.6 copy.83
  123.0 2.1 copy_convert_fusion
  125.1 2.5 copy.53
  127.7 3.6 %all-to-all-done = bf16[512,4,512]{2,1,0:T(4,128)(2,1)S(1)} async-done(((bf16[512,4,512]{2,1,0:T(4,128)(2,1)}), bf16[512,4,512]{2,1,0:T(4,128)(2,1)S(1)}, u32[]{:S(2)}, u32[]{:S(2)}) %all-to-all-start) | async-done | bytes 2097184 | tf_op jit(solution)/shard_map/all_to_all | solution.py:40
  131.3 1.3 copy-done
  132.6 4.5 %all-to-all-start.3 = ((bf16[512,4,512]{2,1,0:T(4,128)(2,1)}), bf16[512,4,512]{2,1,0:T(4,128)(2,1)}, u32[]{:S(2)}, u32[]{:S(2)}) async-start(bf16[512,4,512]{2,1,0:T(4,128)(2,1)} %scatter_fusion.2), calls=%async_computation.3 | async-start | bytes 4194304 | tf_op jit(solution)/shard_map/all_to_all | solution.py:41
  137.3 3.0 copy.49
  140.3 14.7 %bitcast_reduce_fusion = (f32[512,4,4]{0,2,1:T(4,128)S(1)}, f32[4,512,4,1024]{3,1,2,0:T(8,128)}) fusion(bf16[512,4,4,128]{0,3,2,1:T(8,128)(2,1)S(1)} %bitcast.110, bf16[1,4,1024,128]{3,2,1,0:T(8,128)(2,1)} %all-gather.5.cloned.1.call-done), kind=kOutput, calls=%fused_computation.9 | convolution fusion | flops 2164252672 | bytes 36732928 | tf_op jit(solution)/shard_map/while/body/eval_jaxpr/nkgd,ksd->nkgs/dot_general | solution.py:63
  155.0 14.2 %fusion.5 = f32[512,4,4]{0,2,1:T(4,128)S(1)} fusion(f32[4,512,4,1024]{3,1,2,0:T(8,128)} %get-tuple-element.74, f32[512,4,4]{0,2,1:T(4,128)S(1)} %get-tuple-element.73), kind=kLoop, calls=%fused_computation.13 | loop fusion | flops 25157632 | bytes 33619968 | tf_op jit(solution)/shard_map/while/body/eval_jaxpr/reduce_sum | solution.py:70
  169.2 15.6 %all-to-all-done.3 = bf16[512,4,512]{2,1,0:T(4,128)(2,1)} async-done(((bf16[512,4,512]{2,1,0:T(4,128)(2,1)}), bf16[512,4,512]{2,1,0:T(4,128)(2,1)}, u32[]{:S(2)}, u32[]{:S(2)}) %all-to-all-start.3) | async-done | bytes 2097184 | tf_op jit(solution)/shard_map/all_to_all | solution.py:41
  184.9 4.3 %copy.55 = bf16[512,4,512]{0,2,1:T(8,128)(2,1)} copy(bf16[512,4,512]{2,1,0:T(4,128)(2,1)} %all-to-all-done.3) | data formatting | bytes 4194304 | tf_op jit(solution)/shard_map/all_to_all | solution.py:41
  189.7 16.0 %multiply_reduce_fusion.1 = (f32[512,4,4]{0,2,1:T(4,128)S(1)}, bf16[512,4,4,128]{0,3,2,1:T(8,128)(2,1)}) fusion(f32[512,4,128]{0,2,1:T(8,128)} %copy.53, f32[512,4,4]{0,2,1:T(4,128)S(1)} %get-tuple-element.70, bf16[512,4,512]{0,2,1:T(8,128)(2,1)} %copy.55, bf16[1,4,1024,128]{2,3,1,0:T(8,128)(2,1)} %all-gather.7.cloned.1.call-done, ...), kind=kOutput, calls=%fused_computation.23 | convolution fusion | flops 2187321344 | bytes 39976960 | tf_op jit(solution)/shard_map/while/body/eval_jaxpr/nkgs,ksd->nkgd/dot_general | solution.py:86
  205.8 22.0 %bitcast_multiply_fusion = f32[4,1024,128]{2,1,0:T(8,128)} fusion(bf16[512,4,4,128]{0,3,2,1:T(8,128)(2,1)S(1)} %bitcast.111, f32[512,4,4]{0,2,1:T(4,128)S(1)} %get-tuple-element.54, bf16[512,4,4,128]{0,3,2,1:T(8,128)(2,1)} %bitcast.114, bf16[1,4,1024,128]{2,3,1,0:T(8,128)(2,1)S(1)} %copy-done.10, f32[4,512,4,1024]{3,1,2,0:T(8,128)} %get-tuple-element.74, ...), kind=kOutput, calls=%fused_computation.29 | convolution fusion | flops 4345823232 | bytes 40992768 | tf_op jit(solution)/shard_map/while/body/eval_jaxpr/nkgs,nkgd->ksd/dot_general | solution.py:104
  228.1 1.3 copy-done.5
  229.4 16.3 %fusion.17 = f32[4,1024,128]{2,1,0:T(8,128)} fusion(bf16[512,4,4,128]{0,3,2,1:T(8,128)(2,1)S(1)} %bitcast.115, f32[4,512,4,1024]{3,1,2,0:T(8,128)} %get-tuple-element.74, f32[512,4,4]{0,2,1:T(4,128)S(1)} %get-tuple-element.71, f32[512,4,4]{0,2,1:T(4,128)S(1)} %get-tuple-element.72), kind=kOutput, calls=%fused_computation.31 | convolution fusion | flops 2181038080 | bytes 37814272 | tf_op jit(solution)/shard_map/while/body/eval_jaxpr/nkgs,nkgd->ksd/dot_general | solution.py:107
  245.7 1.6 copy-done.6
  247.2 3.1 copy.54
  250.3 3.8 %all-to-all-start.2 = ((bf16[512,4,512]{2,1,0:T(4,128)(2,1)}), bf16[512,4,512]{2,1,0:T(4,128)(2,1)S(1)}, u32[]{:S(2)}, u32[]{:S(2)}) async-start(bf16[512,4,512]{2,1,0:T(4,128)(2,1)} %copy.54), calls=%async_computation.2 | async-start | bytes 4194304 | tf_op jit(solution)/shard_map/all_to_all | solution.py:124
  254.1 47.6 %all-to-all-done.2 = bf16[512,4,512]{2,1,0:T(4,128)(2,1)S(1)} async-done(((bf16[512,4,512]{2,1,0:T(4,128)(2,1)}), bf16[512,4,512]{2,1,0:T(4,128)(2,1)S(1)}, u32[]{:S(2)}, u32[]{:S(2)}) %all-to-all-start.2) | async-done | bytes 2097184 | tf_op jit(solution)/shard_map/all_to_all | solution.py:124
  301.7 2.4 gather_fusion
  304.2 6.5 %maximum_subtract_fusion = (f32[2,1,4,512,128]{4,3,2,1,0:T(8,128)S(1)}, f32[2,1,4,512,128]{4,3,2,1,0:T(8,128)}, f32[2,1,4,512,128]{4,3,2,1,0:T(8,128)}) fusion(f32[1,1,4,512,128]{4,3,2,1,0:T(8,128)} %bitcast.113, f32[1,1,4,512,128]{4,3,2,1,0:T(8,128)S(1)} %bitcast.112, f32[1,1,4,512,128]{4,3,2,1,0:T(8,128)} %bitcast.118, ...), kind=kLoop, calls=%fused_computation.27 | loop fusion | flops 6815744 | bytes 14680064 | tf_op jit(solution)/shard_map/sub | solution.py:130
  310.7 1.5 slice_bitcast_fusion
  (48 shorter events, 5.5 us)
Async XLA Ops:
  9.6 79.1 %copy-start.8 = (s32[256,1]{0,1:T(1,128)}, s32[256,1]{0,1:T(1,128)S(1)}, u32[]{:S(2)}) copy-start(s32[256,1]{0,1:T(1,128)S(1)} %compare_select_fusion) | copy-start | bytes 3076
  40.5 8.3 %copy-start.7 = (bf16[256,4,512]{2,1,0:T(4,128)(2,1)S(1)}, bf16[256,4,512]{2,1,0:T(4,128)(2,1)}, u32[]{:S(2)}) copy-start(bf16[256,4,512]{2,1,0:T(4,128)(2,1)} %param.9) | copy-start | bytes 3145732
  40.5 37.1 %all-to-all-start.1 = ((bf16[512,4,256]{2,1,0:T(4,128)(2,1)}), bf16[512,4,256]{2,1,0:T(4,128)(2,1)S(1)}, u32[]{:S(2)}, u32[]{:S(2)}) async-start(bf16[512,4,256]{2,1,0:T(4,128)(2,1)} %scatter_fusion.1), calls=%async_computation.1 | async-start | bytes 2097152 | tf_op jit(solution)/shard_map/all_to_all | solution.py:42
  77.6 6.1 %copy-start.1 = (f32[1,4,512,128]{3,2,1,0:T(8,128)S(1)}, f32[1,4,512,128]{3,2,1,0:T(8,128)}, u32[]{:S(2)}) copy-start(f32[1,4,512,128]{3,2,1,0:T(8,128)} %param.14) | copy-start | bytes 3145732
  77.6 1.0 copy-start.3
  78.6 52.7 %all-to-all-start = ((bf16[512,4,512]{2,1,0:T(4,128)(2,1)}), bf16[512,4,512]{2,1,0:T(4,128)(2,1)S(1)}, u32[]{:S(2)}, u32[]{:S(2)}) async-start(bf16[512,4,512]{2,1,0:T(4,128)(2,1)} %scatter_fusion), calls=%async_computation | async-start | bytes 4194304 | tf_op jit(solution)/shard_map/all_to_all | solution.py:40
  83.7 56.6 %all-gather.5.cloned.1.call-start = ((), (), s32[]{:S(2)}) async-start(), calls=%async_computation.8 | async-start | bytes 1572864 | tf_op jit(solution)/shard_map/all_gather | solution.py:48
  84.5 105.1 %all-gather.7.cloned.1.call-start = ((), (), s32[]{:S(2)}) async-start(), calls=%async_computation.9 | async-start | bytes 1572864 | tf_op jit(solution)/shard_map/all_gather | solution.py:49
  88.7 31.3 %copy-start.4 = (bf16[512,4,256]{2,1,0:T(4,128)(2,1)S(1)}, bf16[512,4,256]{2,1,0:T(4,128)(2,1)}, u32[]{:S(2)}) copy-start(bf16[512,4,256]{2,1,0:T(4,128)(2,1)} %copy-done.3) | copy-start | bytes 3145732
  131.3 1.3 copy-start
  132.6 52.3 %all-to-all-start.3 = ((bf16[512,4,512]{2,1,0:T(4,128)(2,1)}), bf16[512,4,512]{2,1,0:T(4,128)(2,1)}, u32[]{:S(2)}, u32[]{:S(2)}) async-start(bf16[512,4,512]{2,1,0:T(4,128)(2,1)} %scatter_fusion.2), calls=%async_computation.3 | async-start | bytes 4194304 | tf_op jit(solution)/shard_map/all_to_all | solution.py:41
  137.1 167.1 %reduce-scatter.3.cloned.1.call-start = ((), (), s32[]{:S(2)}) async-start(), calls=%async_computation.6 | async-start | bytes 3145728 | tf_op jit(solution)/shard_map/reduce_scatter | solution.py:121
  189.7 16.1 %copy-start.10 = (bf16[1,4,1024,128]{2,3,1,0:T(8,128)(2,1)S(1)}, bf16[1,4,1024,128]{2,3,1,0:T(8,128)(2,1)}, u32[]{:S(2)}) copy-start(bf16[1,4,1024,128]{2,3,1,0:T(8,128)(2,1)} %all-gather.7.cloned.1.call-done) | copy-start | bytes 3145732
  227.8 1.6 copy-start.5
  227.8 76.4 %reduce-scatter.5.cloned.1.call-start = ((), (), s32[]{:S(2)}) async-start(), calls=%async_computation.7 | async-start | bytes 3145728 | tf_op jit(solution)/shard_map/reduce_scatter | solution.py:122
  245.6 1.6 copy-start.6
  250.3 3.8 %copy-start.9 = (s32[256,1]{0,1:T(1,128)S(1)}, s32[256,1]{0,1:T(1,128)}, u32[]{:S(2)}) copy-start(s32[256,1]{0,1:T(1,128)} %copy-done.8) | copy-start | bytes 3076
  250.3 51.4 %all-to-all-start.2 = ((bf16[512,4,512]{2,1,0:T(4,128)(2,1)}), bf16[512,4,512]{2,1,0:T(4,128)(2,1)S(1)}, u32[]{:S(2)}, u32[]{:S(2)}) async-start(bf16[512,4,512]{2,1,0:T(4,128)(2,1)} %copy.54), calls=%async_computation.2 | async-start | bytes 4194304 | tf_op jit(solution)/shard_map/all_to_all | solution.py:124
  254.1 50.1 %copy-start.2 = (f32[1,4,512,128]{3,2,1,0:T(8,128)S(1)}, f32[1,4,512,128]{3,2,1,0:T(8,128)}, u32[]{:S(2)}) copy-start(f32[1,4,512,128]{3,2,1,0:T(8,128)} %param.14) | copy-start | bytes 3145732
Sparse Core Ops, SparseCore 0:
  86.6 10.5 all-gather.4
  98.7 10.1 all-gather.6
  227.9 8.7 reduce-scatter.2
  245.8 8.5 reduce-scatter.4
where the time goes:
time: 322 us; the launch traced here: 319 us
  local copies, waits for them, and re-layouts  121 us (38%)
  matrix products  69 us (21%)
  waiting for transfers between devices  67 us (21%)
  other arithmetic  27.8 us (9%)
  starting transfers between devices  20.3 us (6%)
  between operations  13.9 us (4%)
    scatter x3, local copies, waits for them, and re-layouts, pack(): return jnp.zeros((n_owner * cap,) + x.shape[1:], x.dtype).at[place].set(x)  89.7 us
    all_to_all x1, waiting for transfers between devices, per_device(): lax.all_to_all(answer_rows, 'owner', split_axis=0, concat_axis=0, tiled=T...  47.6 us
    dot_general x1, matrix products, backward(): jnp.einsum('nkgs,nkgd->ksd', dweights, q_block, preferred_element_type=jn...  22 us
    dot_general x1, matrix products, backward(): jnp.einsum('nkgs,nkgd->ksd', weights, c_block, preferred_element_type=jnp...  16.3 us
    dot_general x1, matrix products, weighted(): jnp.einsum('nkgs,ksd->nkgd', prob.astype(jnp.bfloat16), val_use, preferre...  16 us
    all_to_all x1, waiting for transfers between devices, per_device(): lax.all_to_all(pack(cotangent), 'owner', split_axis=0, concat_axis=0, til...  15.6 us
    dot_general x1, matrix products, scores_of(): jnp.einsum('nkgd,ksd->nkgs', q_block, key_use, preferred_element_type=jnp...  14.7 us
    reduce_sum x1, other arithmetic, stats(): return (local_top, jnp.sum(jnp.exp(score - local_top[..., None]), axis=-1))  14.2 us
  transfers between devices with their start and end apart: 8, of which 3 were waited for; matrix products, arithmetic and copies ran while one was open for 42% of the time, Pallas kernels for 0%

commit v1 on v0

v1 whole, which is shorter than its diff:
```python
import functools

import jax
import jax.numpy as jnp
from jax import lax
from jax.experimental import pallas as pl
from jax.experimental.pallas import tpu as pltpu
from jax.sharding import PartitionSpec as P

MESH = pl.DeviceIdType.MESH


def dot(a, b, ca, cb):
    return lax.dot_general(a, b, (((ca,), (cb,)), ((), ())), preferred_element_type=jnp.float32)


def kernel(
    n,
    cap,
    owner_of,
    tables,
    queries,
    cotangent,
    own_kv,
    keys,
    values,
    attended,
    grad,
    cache,
    stash,
    local,
    half_out,
    half_in,
    chain_in,
    pf_send,
    pf_recv,
    zf_send,
    zf_recv,
    pb_send,
    pb_recv,
    zb_send,
    zb_recv,
):
    z = lax.axis_index("owner")
    r = lax.axis_index("rep")
    heads, tokens, width = queries.shape
    dh = keys.shape[2]
    slots = keys.shape[1]
    groups = width // dh
    scale = dh ** (-0.5)
    is_end = jnp.logical_or(z == 0, z == n - 1)
    bf16 = jnp.bfloat16
    f32 = jnp.float32

    def to_partner(src, dst, s_sem, r_sem):
        return pltpu.make_async_remote_copy(
            src_ref=src, dst_ref=dst, send_sem=s_sem, recv_sem=r_sem,
            device_id={"rep": 1 - r}, device_id_type=MESH,
        )

    def to_owner(src, dst, s_sem, r_sem, where):
        return pltpu.make_async_remote_copy(
            src_ref=src, dst_ref=dst, send_sem=s_sem, recv_sem=r_sem,
            device_id={"owner": where}, device_id_type=MESH,
        )

    def share_half(t, h):
        return to_partner(cache.at[t, h, r], cache.at[t, h, r], pf_send.at[t, h], pf_recv.at[t, h])

    def pass_on(t, h, step):
        return to_owner(
            cache.at[t, h, r], cache.at[t, h, r],
            zf_send.at[(step + 1) // 2, t, h], zf_recv.at[t, h], z + step,
        )

    def share_grad(t, h):
        return to_partner(half_out.at[t, h], half_in.at[t, h], pb_send.at[t, h], pb_recv.at[t, h])

    def chain(t, h, step):
        slot = t if step == 1 else jnp.where(t == z + step, n, t)
        return to_owner(
            half_in.at[t, h], chain_in.at[slot, h], zb_send.at[t, h], zb_recv.at[slot, h], z + step
        )

    barrier = pltpu.get_barrier_semaphore()
    pl.semaphore_signal(barrier, inc=1, device_id={"rep": 1 - r}, device_id_type=MESH)

    @pl.when(z > 0)
    def _():
        pl.semaphore_signal(barrier, inc=1, device_id={"owner": z - 1}, device_id_type=MESH)

    @pl.when(z < n - 1)
    def _():
        pl.semaphore_signal(barrier, inc=1, device_id={"owner": z + 1}, device_id_type=MESH)

    def cast(h, carry):
        cache[z, h, r, 0] = keys[h].astype(bf16)
        cache[z, h, r, 1] = values[h].astype(bf16)
        return carry

    lax.fori_loop(0, heads, cast, 0)
    peers = 1 + jnp.where(z > 0, 1, 0) + jnp.where(z < n - 1, 1, 0)
    pl.semaphore_wait(barrier, peers)

    def first(h, carry):
        @pl.when(z > 0)
        def _():
            pass_on(z, h, -1).start()

        @pl.when(z < n - 1)
        def _():
            pass_on(z, h, 1).start()

        share_half(z, h).start()
        return carry

    lax.fori_loop(0, heads, first, 0)

    dest = jnp.zeros((1, tokens), jnp.int32)
    for i in range(owner_of.shape[0]):
        dest = jnp.where(tables[...] == i, owner_of[i], dest)
    earlier = (
        lax.broadcasted_iota(jnp.int32, (tokens, tokens), 0)
        < lax.broadcasted_iota(jnp.int32, (tokens, tokens), 1)
    ).astype(f32).astype(bf16)
    attended[...] = jnp.zeros(attended.shape, attended.dtype)

    def receive(pair, side):
        d = 1 + pair // heads
        h = lax.rem(pair, heads)
        t = z - d if side == 0 else z + d
        there = t >= 0 if side == 0 else t < n

        @pl.when(jnp.logical_and(jnp.logical_and(pair >= 0, pair < (n - 1) * heads), there))
        def _():
            pass_on(t, h, 1 if side == 0 else -1).wait_recv()

            if side == 0:
                @pl.when(z < n - 1)
                def _():
                    pass_on(t, h, 1).start()
            else:
                @pl.when(z > 0)
                def _():
                    pass_on(t, h, -1).start()

            share_half(t, h).start()

    def compute(t, h):
        share_half(t, h).wait_recv()
        hit = dest == t
        hits = jnp.broadcast_to(hit.astype(f32), (8, tokens)).astype(bf16)
        rank = dot(hits, earlier, 1, 0)[:1].astype(jnp.int32)
        pick = jnp.logical_and(
            lax.broadcasted_iota(jnp.int32, (cap, tokens), 0) == rank, hit
        ).astype(f32).astype(bf16)

        def rows(x):
            return jnp.concatenate([x[:, g * dh:(g + 1) * dh] for g in range(groups)], axis=0)

        q = rows(dot(pick, queries[h], 1, 0))
        c = rows(dot(pick, cotangent[h], 1, 0))
        kv = dot(pick, own_kv[h], 1, 0)
        kself = jnp.concatenate([kv[:, :dh]] * groups, axis=0)
        vself = jnp.concatenate([kv[:, dh:]] * groups, axis=0)
        own = jnp.sum(jnp.transpose(q * kself), axis=0, keepdims=True) * scale
        qb = q.astype(bf16)
        cb = c.astype(bf16)
        k = cache[t, h, :, 0].reshape(2 * slots, dh)
        v = cache[t, h, :, 1].reshape(2 * slots, dh)
        score = dot(k, qb, 1, 1) * scale
        top = jnp.maximum(jnp.max(score, axis=0, keepdims=True), own)
        expo = jnp.exp(score - top)
        self_exp = jnp.exp(own - top)
        total = jnp.sum(expo, axis=0, keepdims=True) + self_exp
        inv = 1.0 / total
        prob = expo * inv
        self_weight = (self_exp * inv).astype(bf16).astype(f32)
        weights = prob.astype(bf16)
        out = dot(v, weights, 0, 0) + self_weight * jnp.transpose(vself)
        delta = jnp.sum(jnp.transpose(c) * out, axis=0, keepdims=True)
        dprob = dot(v, cb, 1, 1)
        dweights = (prob * (dprob - delta)).astype(bf16)
        gk = dot(dweights, qb, 1, 0) * scale
        gv = dot(weights, cb, 1, 0)
        for i in range(2):
            local[i, 0] = gk[i * slots:(i + 1) * slots]
            local[i, 1] = gv[i * slots:(i + 1) * slots]
        half_out[t, h] = local[1 - r].astype(bf16)
        share_grad(t, h).start()
        stash[t, h] = local[r]
        answer = jnp.transpose(out).astype(bf16)
        answer = jnp.concatenate([answer[g * cap:(g + 1) * cap] for g in range(groups)], axis=1)
        attended[h] = (attended[h].astype(f32) + dot(pick, answer, 0, 0)).astype(bf16)

    def finish(pair, right):
        level = 1 + pair // heads
        h = lax.rem(pair, heads)
        t = level if right else n - 1 - level
        there = t > z if right else t < z
        step = 1 if right else -1

        @pl.when(jnp.logical_and(jnp.logical_and(pair >= 0, pair < (n - 1) * heads), there))
        def _():
            share_grad(t, h).wait_recv()

            @pl.when(z > 0 if right else z < n - 1)
            def _():
                to_owner(
                    half_in.at[t, h], chain_in.at[t, h], zb_send.at[t, h], zb_recv.at[t, h],
                    z - step,
                ).wait_recv()
                stash[t, h] = stash[t, h] + chain_in[t, h].astype(f32)

            half_in[t, h] = (stash[t, h] + half_in[t, h].astype(f32)).astype(bf16)
            chain(t, h, step).start()

    def body(m, carry):
        pair = m - jnp.where(is_end, heads - 1, 0)
        receive(pair, 0)
        receive(pair, 1)

        def one(side, carry):
            d = m // heads
            h = lax.rem(m, heads)
            t = z - d + 2 * d * side
            there = jnp.logical_and(jnp.logical_and(t >= 0, t < n), jnp.logical_or(d > 0, side == 0))

            @pl.when(jnp.logical_and(there, m < n * heads))
            def _():
                compute(t, h)

            return carry

        lax.fori_loop(0, 2, one, 0)
        done = m - heads - jnp.where(is_end, 1, 0)

        @pl.when(2 * z < n - 1)
        def _():
            finish(done, True)
            finish(done, False)

        @pl.when(2 * z >= n - 1)
        def _():
            finish(done, False)
            finish(done, True)

        return carry

    lax.fori_loop(0, n * heads + 1, body, 0)

    def last(h, carry):
        share_grad(z, h).wait_recv()
        total = stash[z, h] + half_in[z, h].astype(f32)
        stash[z, h] = total

        @pl.when(z > 0)
        def _():
            to_owner(
                half_in.at[z, h], chain_in.at[z, h], zb_send.at[z, h], zb_recv.at[z, h], z - 1
            ).wait_recv()
            stash[z, h] = stash[z, h] + chain_in[z, h].astype(f32)

        @pl.when(z < n - 1)
        def _():
            to_owner(
                half_in.at[z, h], chain_in.at[n, h], zb_send.at[z, h], zb_recv.at[n, h], z + 1
            ).wait_recv()
            stash[z, h] = stash[z, h] + chain_in[n, h].astype(f32)

        grad[0, h] = stash[z, h, 0]
        grad[1, h] = stash[z, h, 1]
        return carry

    lax.fori_loop(0, heads, last, 0)

    def drain(i, carry):
        t = i // heads
        h = lax.rem(i, heads)
        share_half(t, h).wait_send()
        share_grad(t, h).wait_send()

        @pl.when(jnp.logical_and(t <= z, z < n - 1))
        def _():
            pass_on(t, h, 1).wait_send()

        @pl.when(jnp.logical_and(t >= z, z > 0))
        def _():
            pass_on(t, h, -1).wait_send()

        @pl.when(t > z)
        def _():
            chain(t, h, 1).wait_send()

        @pl.when(t < z)
        def _():
            chain(t, h, -1).wait_send()

        return carry

    lax.fori_loop(0, n * heads, drain, 0)


def attend(n, owner_of, tables, queries, cotangent, own_kv, keys, values):
    heads, tokens, width = queries.shape
    slots, dh = keys.shape[1:]
    cap = 2 * tokens // n
    vmem = pl.BlockSpec(memory_space=pltpu.VMEM)
    dma = pltpu.SemaphoreType.DMA
    bf16 = jnp.bfloat16
    piece = (heads, 2, slots, dh)
    return pl.pallas_call(
        functools.partial(kernel, n, cap),
        out_shape=(
            jax.ShapeDtypeStruct((heads, tokens, width), bf16),
            jax.ShapeDtypeStruct((2, heads, slots, dh), jnp.float32),
        ),
        in_specs=[pl.BlockSpec(memory_space=pltpu.SMEM)] + [vmem] * 6,
        out_specs=(vmem, vmem),
        scratch_shapes=[
            pltpu.VMEM((n, heads, 2, 2, slots, dh), bf16),
            pltpu.VMEM((n,) + piece, jnp.float32),
            pltpu.VMEM((2, 2, slots, dh), jnp.float32),
            pltpu.VMEM((n,) + piece, bf16),
            pltpu.VMEM((n,) + piece, bf16),
            pltpu.VMEM((n + 1,) + piece, bf16),
            dma((n, heads)),
            dma((n, heads)),
            dma((2, n, heads)),
            dma((n, heads)),
            dma((n, heads)),
            dma((n, heads)),
            dma((n, heads)),
            dma((n + 1, heads)),
        ],
        compiler_params=pltpu.CompilerParams(
            collective_id=0, has_side_effects=True, vmem_limit_bytes=62 * 1024 * 1024
        ),
    )(owner_of, tables, queries, cotangent, own_kv, keys, values)


def per_device(
    queries,
    cotangent,
    own_kv,
    tables,
    table_owner,
    cache_keys,
    cache_values,
    first_moment,
    second_moment,
):
    n = lax.axis_size("owner")
    attended, grad = attend(
        n,
        table_owner,
        tables.reshape(1, -1),
        jnp.swapaxes(queries, 0, 1),
        jnp.swapaxes(cotangent, 0, 1),
        jnp.swapaxes(own_kv, 0, 1),
        cache_keys[0],
        cache_values[0],
    )
    attended = jnp.swapaxes(attended, 0, 1)
    grad = grad[:, None]
    new_first = 0.9 * first_moment + 0.1 * grad
    new_second = 0.95 * second_moment + 0.05 * grad * grad
    step = 0.02 * new_first / (jnp.sqrt(new_second) + 1e-08)
    return (attended, cache_keys - step[0], cache_values - step[1], new_first, new_second)


def solution(mesh):
    in_specs = (
        P(("groups", "owner", "rep"), "head", None),
        P(("groups", "owner", "rep"), "head", None),
        P(("groups", "owner", "rep"), "head", None),
        P(("groups", "owner", "rep"), None),
        P("groups"),
        P(("groups", "owner"), "head", "rep", None),
        P(("groups", "owner"), "head", "rep", None),
        P(None, ("groups", "owner"), "head", "rep", None),
        P(None, ("groups", "owner"), "head", "rep", None),
    )
    out_specs = (
        P(("groups", "owner", "rep"), "head", None),
        P(("groups", "owner"), "head", "rep", None),
        P(("groups", "owner"), "head", "rep", None),
        P(None, ("groups", "owner"), "head", "rep", None),
        P(None, ("groups", "owner"), "head", "rep", None),
    )
    return jax.shard_map(
        per_device, mesh=mesh, in_specs=in_specs, out_specs=out_specs, check_vma=False
    )
```

time: 322 us -> 135 us (0.42); the launches traced: 319 us -> 135 us
  Pallas kernels: 0 us -> 119 us
  local copies, waits for them, and re-layouts: 121 us -> 8.35 us
  matrix products: 69 us -> 0 us
  waiting for transfers between devices: 67 us -> 0 us
  other arithmetic: 27.8 us -> 7.14 us
  starting transfers between devices: 20.3 us -> 0 us
  between operations: 13.9 us -> 0.65 us
    pallas_call x0 -> x1, Pallas kernels: none -> 119 us  [attend(): pl.pallas_call(functools.partial(kernel, n, cap), out_shape=(jax.ShapeDty...]
    scatter x3 -> x0, local copies, waits for them, and re-layouts: 89.7 us -> none  [pack(): return jnp.zeros((n_owner * cap,) + x.shape[1:], x.dtype).at[place].set(x)]
    dot_general x4 -> x0, matrix products: 69 us -> none  [the longest x1 22 us: backward(): jnp.einsum('nkgs,nkgd->ksd', dweights, q_block, preferred_element_type=jn...]
    all_to_all x4 -> x0, waiting for transfers between devices: 66.9 us -> none  [the longest x1 47.6 us: per_device(): lax.all_to_all(answer_rows, 'owner', split_axis=0, concat_axis=0, tiled=T...]
    all_to_all x4 -> x0, starting transfers between devices: 19.8 us -> none  [the longest x1 6.48 us: per_device(): lax.all_to_all(pack(own_kv), 'owner', split_axis=0, concat_axis=0, tiled=...]
    reduce_sum x3 -> x0, other arithmetic: 15 us -> none  [the longest x1 14.2 us: stats(): return (local_top, jnp.sum(jnp.exp(score - local_top[..., None]), axis=-1))]
    all_to_all x2 -> x0, local copies, waits for them, and re-layouts: 7.22 us -> none  [the longest x1 4.25 us: per_device(): lax.all_to_all(pack(cotangent), 'owner', split_axis=0, concat_axis=0, til...]
    convert_element_type x2 -> x0, local copies, waits for them, and re-layouts: 5.59 us -> none  [the longest x1 3.06 us: per_device(): answer_rows = out.astype(jnp.bfloat16).reshape(count, heads, width)]
  transfers between devices with their start and end apart: 8 -> 0, of which waited for: 3 -> 0; matrix products, arithmetic and copies ran while one was open for 42% -> 0% of each run, Pallas kernels for 0% -> 0%
where the time goes in v1:
time: 135 us
  Pallas kernels  119 us (88%)
  local copies, waits for them, and re-layouts  8.35 us (6%)
  other arithmetic  7.14 us (5%)
    pallas_call x1, Pallas kernels, attend(): pl.pallas_call(functools.partial(kernel, n, cap), out_shape=(jax.ShapeDty...  119 us
    unnamed x1, other arithmetic  5.61 us
    unnamed x8, local copies, waits for them, and re-layouts  5.07 us
    transpose x1, local copies, waits for them, and re-layouts, per_device(): jnp.swapaxes(cotangent, 0, 1)  3.27 us

profile of v1, /device:TPU:0, one launch (start us, length us, event | category | flops | bytes accessed | tf_op | source)
XLA Modules:
  0.0 134.9 jit_solution(9503058634257653782)
XLA Ops:
  0.6 1.9 %copy.25 = bf16[256,4,256]{2,0,1:T(8,128)(2,1)} copy(bf16[256,4,256]{2,1,0:T(4,128)(2,1)} %param.11) | data formatting | bytes 1048576 | tf_op args[2]
  2.5 3.3 %copy_bitcast_fusion = (bf16[4,256,512]{2,1,0:T(8,128)(2,1)}, bf16[4,256,512]{2,1,0:T(8,128)(2,1)}) fusion(bf16[256,4,512]{2,1,0:T(4,128)(2,1)} %param.10, bf16[256,4,512]{2,1,0:T(4,128)(2,1)} %param.9), kind=kLoop, calls=%fused_computation.11 | loop fusion | bytes 4194304 | tf_op jit(solution)/shard_map/transpose | solution.py:359
  5.8 118.8 %shard_map.128 = (bf16[4,256,512]{2,1,0:T(8,128)(2,1)}, f32[2,4,512,128]{3,2,1,0:T(8,128)}) custom-call(s32[4]{0:T(128)} %owner_of.1, s32[1,256]{1,0:T(1,128)} %bitcast.57, bf16[4,256,512]{2,1,0:T(8,128)(2,1)} %get-tuple-element.20.queries, bf16[4,256,512]{2,1,0:T(8,128)(2,1)} %get-tuple-element.19.cotangent, bf16[4,256,256]{2,1,0:T(8,128)(2,1)} %bitcast.55, ...), custom_call_target="tpu_custom_call" | custom-call | tf_op jit(solution)/shard_map/pallas_call | solution.py:312
  124.6 0.0 copy-start.2
  124.6 3.2 %copy.19 = bf16[256,4,512]{2,1,0:T(4,128)(2,1)} copy(bf16[256,4,512]{2,0,1:T(8,128)(2,1)} %bitcast.56) | data formatting | bytes 2097152
  127.8 0.0 copy-done.2
  127.8 0.0 copy-start
  127.8 0.0 copy-start.1
  127.8 5.6 %fusion.5 = (f32[2,1,4,512,128]{4,3,2,1,0:T(8,128)}, f32[2,1,4,512,128]{4,3,2,0,1:T(8,128)S(1)}, f32[2,1,4,512,128]{4,3,2,1,0:T(8,128)}) fusion(f32[2,4,512,128]{3,2,1,0:T(8,128)} %get-tuple-element.8, f32[2,1,4,512,128]{4,3,2,1,0:T(8,128)S(1)} %copy-done.2, f32[2,1,4,512,128]{4,3,2,1,0:T(8,128)} %param.16), kind=kLoop, calls=%fused_computation.15 | loop fusion | flops 5242880 | bytes 12582912
  133.4 0.0 copy-done
  133.4 0.0 copy-done.1
  133.4 1.5 %fusion.2 = (f32[1,4,512,128]{3,2,1,0:T(8,128)}, f32[1,4,512,128]{3,2,1,0:T(8,128)}) fusion(f32[1,4,512,128]{3,2,1,0:T(8,128)S(1)} %copy-done.1, f32[2,1,4,512,128]{4,3,2,0,1:T(8,128)S(1)} %get-tuple-element.15, f32[1,4,512,128]{3,2,1,0:T(8,128)S(1)} %copy-done), kind=kLoop, calls=%fused_computation.8 | loop fusion | flops 524288 | bytes 6291456 | tf_op jit(solution)/shard_map/sub | solution.py:369
Async XLA Ops:
  124.6 3.2 %copy-start.2 = (f32[2,1,4,512,128]{4,3,2,1,0:T(8,128)S(1)}, f32[2,1,4,512,128]{4,3,2,1,0:T(8,128)}, u32[]{:S(2)}) copy-start(f32[2,1,4,512,128]{4,3,2,1,0:T(8,128)} %param.17) | copy-start | bytes 6291460
  127.8 5.6 %copy-start = (f32[1,4,512,128]{3,2,1,0:T(8,128)S(1)}, f32[1,4,512,128]{3,2,1,0:T(8,128)}, u32[]{:S(2)}) copy-start(f32[1,4,512,128]{3,2,1,0:T(8,128)} %param.14) | copy-start | bytes 3145732
  127.8 5.6 %copy-start.1 = (f32[1,4,512,128]{3,2,1,0:T(8,128)S(1)}, f32[1,4,512,128]{3,2,1,0:T(8,128)}, u32[]{:S(2)}) copy-start(f32[1,4,512,128]{3,2,1,0:T(8,128)} %param.15) | copy-start | bytes 3145732

commit v2 on v1

--- a/solution.py
+++ b/solution.py
@@ -19,13 +19,16 @@
     cap,
     owner_of,
     tables,
-    queries,
-    cotangent,
-    own_kv,
+    queries_in,
+    cotangent_in,
+    own_kv_in,
     keys,
     values,
     attended,
     grad,
+    queries,
+    cotangent,
+    own_kv,
     cache,
     stash,
     local,
@@ -46,6 +49,8 @@
     heads, tokens, width = queries.shape
     dh = keys.shape[2]
     slots = keys.shape[1]
+    parts = half_in.shape[2]
+    part = slots // parts
     groups = width // dh
     scale = dh ** (-0.5)
     is_end = jnp.logical_or(z == 0, z == n - 1)
@@ -64,23 +69,31 @@
             device_id={"owner": where}, device_id_type=MESH,
         )
 
-    def share_half(t, h):
-        return to_partner(cache.at[t, h, r], cache.at[t, h, r], pf_send.at[t, h], pf_recv.at[t, h])
-
-    def pass_on(t, h, step):
+    def share_half(t, h, u):
+        return to_partner(
+            cache.at[t, h, r, u], cache.at[t, h, r, u], pf_send.at[t, h, u], pf_recv.at[t, h, u]
+        )
+
+    def pass_on(t, h, u, step):
         return to_owner(
-            cache.at[t, h, r], cache.at[t, h, r],
-            zf_send.at[(step + 1) // 2, t, h], zf_recv.at[t, h], z + step,
-        )
-
-    def share_grad(t, h):
-        return to_partner(half_out.at[t, h], half_in.at[t, h], pb_send.at[t, h], pb_recv.at[t, h])
-
-    def chain(t, h, step):
+            cache.at[t, h, r, u], cache.at[t, h, r, u],
+            zf_send.at[(step + 1) // 2, t, h, u], zf_recv.at[t, h, u], z + step,
+        )
+
+    def share_grad(t, h, u):
+        return to_partner(
+            half_out.at[t, h, u], half_in.at[t, h, u], pb_send.at[t, h, u], pb_recv.at[t, h, u]
+        )
+
+    def chain_to(t, h, u, slot, where):
+        return to_owner(
+            half_in.at[t, h, u], chain_in.at[slot, h, u],
+            zb_send.at[t, h, u], zb_recv.at[slot, h, u], where,
+        )
+
+    def chain(t, h, u, step):
         slot = t if step == 1 else jnp.where(t == z + step, n, t)
-        return to_owner(
-            half_in.at[t, h], chain_in.at[slot, h], zb_send.at[t, h], zb_recv.at[slot, h], z + step
-        )
+        return chain_to(t, h, u, slot, z + step)
 
     barrier = pltpu.get_barrier_semaphore()
     pl.semaphore_signal(barrier, inc=1, device_id={"rep": 1 - r}, device_id_type=MESH)
@@ -94,8 +107,9 @@
         pl.semaphore_signal(barrier, inc=1, device_id={"owner": z + 1}, device_id_type=MESH)
 
     def cast(h, carry):
-        cache[z, h, r, 0] = keys[h].astype(bf16)
-        cache[z, h, r, 1] = values[h].astype(bf16)
+        for u in range(parts):
+            cache[z, h, r, u, 0] = keys[h, u * part:(u + 1) * part].astype(bf16)
+            cache[z, h, r, u, 1] = values[h, u * part:(u + 1) * part].astype(bf16)
         return carry
 
     lax.fori_loop(0, heads, cast, 0)
@@ -103,19 +117,24 @@
     pl.semaphore_wait(barrier, peers)
 
     def first(h, carry):
-        @pl.when(z > 0)
-        def _():
-            pass_on(z, h, -1).start()
-
-        @pl.when(z < n - 1)
-        def _():
-            pass_on(z, h, 1).start()
-
-        share_half(z, h).start()
+        for u in range(parts):
+            @pl.when(z > 0)
+            def _():
+                pass_on(z, h, u, -1).start()
+
+            @pl.when(z < n - 1)
+            def _():
+                pass_on(z, h, u, 1).start()
+
+            share_half(z, h, u).start()
         return carry
 
     lax.fori_loop(0, heads, first, 0)
 
+    for h in range(heads):
+        queries[h] = queries_in[:, h, :]
+        cotangent[h] = cotangent_in[:, h, :]
+        own_kv[h] = own_kv_in[:, h, :]
     dest = jnp.zeros((1, tokens), jnp.int32)
     for i in range(owner_of.shape[0]):
         dest = jnp.where(tables[...] == i, owner_of[i], dest)
@@ -133,21 +152,23 @@
 
         @pl.when(jnp.logical_and(jnp.logical_and(pair >= 0, pair < (n - 1) * heads), there))
         def _():
-            pass_on(t, h, 1 if side == 0 else -1).wait_recv()
-
-            if side == 0:
-                @pl.when(z < n - 1)
-                def _():
-                    pass_on(t, h, 1).start()
-            else:
-                @pl.when(z > 0)
-                def _():
-                    pass_on(t, h, -1).start()
-
-            share_half(t, h).start()
+            for u in range(parts):
+                pass_on(t, h, u, 1 if side == 0 else -1).wait_recv()
+
+                if side == 0:
+                    @pl.when(z < n - 1)
+                    def _():
+                        pass_on(t, h, u, 1).start()
+                else:
+                    @pl.when(z > 0)
+                    def _():
+                        pass_on(t, h, u, -1).start()
+
+                share_half(t, h, u).start()
 
     def compute(t, h):
-        share_half(t, h).wait_recv()
+        for u in range(parts):
+            share_half(t, h, u).wait_recv()
         hit = dest == t
         hits = jnp.broadcast_to(hit.astype(f32), (8, tokens)).astype(bf16)
         rank = dot(hits, earlier, 1, 0)[:1].astype(jnp.int32)
@@ -166,8 +187,8 @@
         own = jnp.sum(jnp.transpose(q * kself), axis=0, keepdims=True) * scale
         qb = q.astype(bf16)
         cb = c.astype(bf16)
-        k = cache[t, h, :, 0].reshape(2 * slots, dh)
-        v = cache[t, h, :, 1].reshape(2 * slots, dh)
+        k = cache[t, h, :, :, 0].reshape(2 * slots, dh)
+        v = cache[t, h, :, :, 1].reshape(2 * slots, dh)
         score = dot(k, qb, 1, 1) * scale
         top = jnp.maximum(jnp.max(score, axis=0, keepdims=True), own)
         expo = jnp.exp(score - top)
@@ -184,10 +205,13 @@
         gk = dot(dweights, qb, 1, 0) * scale
         gv = dot(weights, cb, 1, 0)
         for i in range(2):
-            local[i, 0] = gk[i * slots:(i + 1) * slots]
-            local[i, 1] = gv[i * slots:(i + 1) * slots]
-        half_out[t, h] = local[1 - r].astype(bf16)
-        share_grad(t, h).start()
+            for u in range(parts):
+                at = i * slots + u * part
+                local[i, u, 0] = gk[at:at + part]
+                local[i, u, 1] = gv[at:at + part]
+        for u in range(parts):
+            half_out[t, h, u] = local[1 - r, u].astype(bf16)
+            share_grad(t, h, u).start()
         stash[t, h] = local[r]
         answer = jnp.transpose(out).astype(bf16)
         answer = jnp.concatenate([answer[g * cap:(g + 1) * cap] for g in range(groups)], axis=1)
@@ -202,18 +226,16 @@
 
         @pl.when(jnp.logical_and(jnp.logical_and(pair >= 0, pair < (n - 1) * heads), there))
         def _():
-            share_grad(t, h).wait_recv()
-
-            @pl.when(z > 0 if right else z < n - 1)
-            def _():
-                to_owner(
-                    half_in.at[t, h], chain_in.at[t, h], zb_send.at[t, h], zb_recv.at[t, h],
-                    z - step,
-                ).wait_recv()
-                stash[t, h] = stash[t, h] + chain_in[t, h].astype(f32)
-
-            half_in[t, h] = (stash[t, h] + half_in[t, h].astype(f32)).astype(bf16)
-            chain(t, h, step).start()
+            for u in range(parts):
+                share_grad(t, h, u).wait_recv()
+
+                @pl.when(z > 0 if right else z < n - 1)
+                def _():
+                    chain_to(t, h, u, t, z - step).wait_recv()
+                    stash[t, h, u] = stash[t, h, u] + chain_in[t, h, u].astype(f32)
+
+                half_in[t, h, u] = (stash[t, h, u] + half_in[t, h, u].astype(f32)).astype(bf16)
+                chain(t, h, u, step).start()
 
     def body(m, carry):
         pair = m - jnp.where(is_end, heads - 1, 0)
@@ -250,26 +272,22 @@
     lax.fori_loop(0, n * heads + 1, body, 0)
 
     def last(h, carry):
-        share_grad(z, h).wait_recv()
-        total = stash[z, h] + half_in[z, h].astype(f32)
-        stash[z, h] = total
-
-        @pl.when(z > 0)
-        def _():
-            to_owner(
-                half_in.at[z, h], chain_in.at[z, h], zb_send.at[z, h], zb_recv.at[z, h], z - 1
-            ).wait_recv()
-            stash[z, h] = stash[z, h] + chain_in[z, h].astype(f32)
-
-        @pl.when(z < n - 1)
-        def _():
-            to_owner(
-                half_in.at[z, h], chain_in.at[n, h], zb_send.at[z, h], zb_recv.at[n, h], z + 1
-            ).wait_recv()
-            stash[z, h] = stash[z, h] + chain_in[n, h].astype(f32)
-
-        grad[0, h] = stash[z, h, 0]
-        grad[1, h] = stash[z, h, 1]
+        for u in range(parts):
+            share_grad(z, h, u).wait_recv()
+            stash[z, h, u] = stash[z, h, u] + half_in[z, h, u].astype(f32)
+
+            @pl.when(z > 0)
+            def _():
+                chain_to(z, h, u, z, z - 1).wait_recv()
+                stash[z, h, u] = stash[z, h, u] + chain_in[z, h, u].astype(f32)
+
+            @pl.when(z < n - 1)
+            def _():
+                chain_to(z, h, u, n, z + 1).wait_recv()
+                stash[z, h, u] = stash[z, h, u] + chain_in[n, h, u].astype(f32)
+
+            grad[0, h, u * part:(u + 1) * part] = stash[z, h, u, 0]
+            grad[1, h, u * part:(u + 1) * part] = stash[z, h, u, 1]
         return carry
 
     lax.fori_loop(0, heads, last, 0)
@@ -277,24 +295,25 @@
     def drain(i, carry):
         t = i // heads
         h = lax.rem(i, heads)
-        share_half(t, h).wait_send()
-        share_grad(t, h).wait_send()
-
-        @pl.when(jnp.logical_and(t <= z, z < n - 1))
-        def _():
-            pass_on(t, h, 1).wait_send()
-
-        @pl.when(jnp.logical_and(t >= z, z > 0))
-        def _():
-            pass_on(t, h, -1).wait_send()
-
-        @pl.when(t > z)
-        def _():
-            chain(t, h, 1).wait_send()
-
-        @pl.when(t < z)
-        def _():
-            chain(t, h, -1).wait_send()
+        for u in range(parts):
+            share_half(t, h, u).wait_send()
+            share_grad(t, h, u).wait_send()
+
+            @pl.when(jnp.logical_and(t <= z, z < n - 1))
+            def _():
+                pass_on(t, h, u, 1).wait_send()
+
+            @pl.when(jnp.logical_and(t >= z, z > 0))
+            def _():
+                pass_on(t, h, u, -1).wait_send()
+
+            @pl.when(t > z)
+            def _():
+                chain(t, h, u, 1).wait_send()
+
+            @pl.when(t < z)
+            def _():
+                chain(t, h, u, -1).wait_send()
 
         return carry
 
@@ -302,13 +321,14 @@
 
 
 def attend(n, owner_of, tables, queries, cotangent, own_kv, keys, values):
-    heads, tokens, width = queries.shape
+    tokens, heads, width = queries.shape
     slots, dh = keys.shape[1:]
     cap = 2 * tokens // n
     vmem = pl.BlockSpec(memory_space=pltpu.VMEM)
     dma = pltpu.SemaphoreType.DMA
     bf16 = jnp.bfloat16
-    piece = (heads, 2, slots, dh)
+    parts = 2
+    piece = (heads, parts, 2, slots // parts, dh)
     return pl.pallas_call(
         functools.partial(kernel, n, cap),
         out_shape=(
@@ -318,20 +338,23 @@
         in_specs=[pl.BlockSpec(memory_space=pltpu.SMEM)] + [vmem] * 6,
         out_specs=(vmem, vmem),
         scratch_shapes=[
-            pltpu.VMEM((n, heads, 2, 2, slots, dh), bf16),
+            pltpu.VMEM((heads, tokens, width), bf16),
+            pltpu.VMEM((heads, tokens, width), bf16),
+            pltpu.VMEM((heads, tokens, 2 * dh), bf16),
+            pltpu.VMEM((n, heads, 2, parts, 2, slots // parts, dh), bf16),
             pltpu.VMEM((n,) + piece, jnp.float32),
-            pltpu.VMEM((2, 2, slots, dh), jnp.float32),
+            pltpu.VMEM((2, parts, 2, slots // parts, dh), jnp.float32),
             pltpu.VMEM((n,) + piece, bf16),
             pltpu.VMEM((n,) + piece, bf16),
             pltpu.VMEM((n + 1,) + piece, bf16),
-            dma((n, heads)),
-            dma((n, heads)),
-            dma((2, n, heads)),
-            dma((n, heads)),
-            dma((n, heads)),
-            dma((n, heads)),
-            dma((n, heads)),
-            dma((n + 1, heads)),
+            dma((n, heads, parts)),
+            dma((n, heads, parts)),
+            dma((2, n, heads, parts)),
+            dma((n, heads, parts)),
+            dma((n, heads, parts)),
+            dma((n, heads, parts)),
+            dma((n, heads, parts)),
+            dma((n + 1, heads, parts)),
         ],
         compiler_params=pltpu.CompilerParams(
             collective_id=0, has_side_effects=True, vmem_limit_bytes=62 * 1024 * 1024
@@ -355,9 +378,9 @@
         n,
         table_owner,
         tables.reshape(1, -1),
-        jnp.swapaxes(queries, 0, 1),
-        jnp.swapaxes(cotangent, 0, 1),
-        jnp.swapaxes(own_kv, 0, 1),
+        queries,
+        cotangent,
+        own_kv,
         cache_keys[0],
         cache_values[0],
     )

time: 135 us -> 129 us (0.956)
  local copies, waits for them, and re-layouts: 8.35 us -> 3.17 us
    transpose x1 -> x0, local copies, waits for them, and re-layouts: 3.27 us -> none  [per_device(): jnp.swapaxes(cotangent, 0, 1)]
    unnamed x8 -> x7, local copies, waits for them, and re-layouts: 5.07 us -> 3.17 us
where the time goes in v2:
time: 129 us
  Pallas kernels  118 us (91%)
  other arithmetic  7.14 us (6%)
  local copies, waits for them, and re-layouts  3.17 us (2%)
    pallas_call x1, Pallas kernels, attend(): pl.pallas_call(functools.partial(kernel, n, cap), out_shape=(jax.ShapeDty...  118 us
    unnamed x1, other arithmetic  5.61 us
    unnamed x7, local copies, waits for them, and re-layouts  3.17 us

profile of v2, /device:TPU:0, one launch (start us, length us, event | category | flops | bytes accessed | tf_op | source)
XLA Modules:
  0.0 129.2 jit_solution(3870980787467839751)
XLA Ops:
  0.6 118.2 %shard_map.128 = (bf16[4,256,512]{2,1,0:T(8,128)(2,1)}, f32[2,4,512,128]{3,2,1,0:T(8,128)}) custom-call(s32[4]{0:T(128)} %owner_of.1, s32[1,256]{1,0:T(1,128)} %bitcast.49, bf16[256,4,512]{2,1,0:T(4,128)(2,1)} %queries_in.1, bf16[256,4,512]{2,1,0:T(4,128)(2,1)} %cotangent_in.1, bf16[256,4,256]{2,1,0:T(4,128)(2,1)} %own_kv_in.1, f32[4,512,128]{2,1,0:T(8,128)} %bitcast.46, ...), custom_call_target="tpu_custom_call" | custom-call | tf_op jit(solution)/shard_map/pallas_call | solution.py:332
  118.8 0.0 copy-start.2
  118.9 3.2 %copy.16 = bf16[256,4,512]{2,1,0:T(4,128)(2,1)} copy(bf16[256,4,512]{2,0,1:T(8,128)(2,1)} %bitcast.48) | data formatting | bytes 2097152
  122.0 0.0 copy-done.2
  122.0 0.0 copy-start
  122.0 0.0 copy-start.1
  122.0 5.6 %fusion.5 = (f32[2,1,4,512,128]{4,3,2,1,0:T(8,128)}, f32[2,1,4,512,128]{4,3,2,0,1:T(8,128)S(1)}, f32[2,1,4,512,128]{4,3,2,1,0:T(8,128)}) fusion(f32[2,4,512,128]{3,2,1,0:T(8,128)} %get-tuple-element.8, f32[2,1,4,512,128]{4,3,2,1,0:T(8,128)S(1)} %copy-done.2, f32[2,1,4,512,128]{4,3,2,1,0:T(8,128)} %param.16), kind=kLoop, calls=%fused_computation.12 | loop fusion | flops 5242880 | bytes 12582912
  127.6 0.0 copy-done
  127.6 0.0 copy-done.1
  127.6 1.5 %fusion.2 = (f32[1,4,512,128]{3,2,1,0:T(8,128)}, f32[1,4,512,128]{3,2,1,0:T(8,128)}) fusion(f32[1,4,512,128]{3,2,1,0:T(8,128)S(1)} %copy-done.1, f32[2,1,4,512,128]{4,3,2,0,1:T(8,128)S(1)} %get-tuple-element.15, f32[1,4,512,128]{3,2,1,0:T(8,128)S(1)} %copy-done), kind=kLoop, calls=%fused_computation.8 | loop fusion | flops 524288 | bytes 6291456 | tf_op jit(solution)/shard_map/sub | solution.py:392
Async XLA Ops:
  118.8 3.2 %copy-start.2 = (f32[2,1,4,512,128]{4,3,2,1,0:T(8,128)S(1)}, f32[2,1,4,512,128]{4,3,2,1,0:T(8,128)}, u32[]{:S(2)}) copy-start(f32[2,1,4,512,128]{4,3,2,1,0:T(8,128)} %param.17) | copy-start | bytes 6291460
  122.0 5.6 %copy-start = (f32[1,4,512,128]{3,2,1,0:T(8,128)S(1)}, f32[1,4,512,128]{3,2,1,0:T(8,128)}, u32[]{:S(2)}) copy-start(f32[1,4,512,128]{3,2,1,0:T(8,128)} %param.14) | copy-start | bytes 3145732
  122.0 5.6 %copy-start.1 = (f32[1,4,512,128]{3,2,1,0:T(8,128)S(1)}, f32[1,4,512,128]{3,2,1,0:T(8,128)}, u32[]{:S(2)}) copy-start(f32[1,4,512,128]{3,2,1,0:T(8,128)} %param.15) | copy-start | bytes 3145732
